TPU v7x, 32 devices: a whole 2x2x4 slice. The times are simulated.
32 devices in a mesh: grp: 2 (over y), mesh: 4 (over z), tm: 2 (over x), rep: 2 (over core).
Axes of the slice: x: 2, y: 2, z: 4, core: 2. Of those that a mesh axis runs over, the one named last changes fastest.
Arguments:
- right_side: float32 [4, 128, 64, 128], P(('grp', 'tm'), ('mesh', 'rep')), parts along dimension 0, may hold values from -25 to 25
- kappa_sq: float32 [256, 64], P(('grp', 'mesh', 'rep')), parts along dimension 0, may hold values from 0.25 to 4
- time_coupling: float32 [2], P('grp'), parts along dimension 0, may hold values from 0.15 to 0.45
- near_stiffness: float32 [128, 64, 384], P(('mesh', 'rep')), may hold values from -0.16 to 0.16, as said below
- far_stiffness: float32 [8, 64, 1536], P(('mesh', 'rep')), may hold values from -0.16 to 0.16, as said below
- near_columns: int32 [128, 6], P(('mesh', 'rep')), may hold values from 0 to 15, as said below
- face_blocks: int32 [8, 6, 4], P(('mesh', 'rep')), may hold values from 0 to 15, as said below
- face_counts: int32 [8, 6], P(('mesh', 'rep')), may hold values from 0 to 4, as said below
Outputs:
- solution_field: float32 [4, 128, 64, 128], P(('grp', 'tm'), ('mesh', 'rep')), parts along dimension 0
- residual: float32 [4, 128, 64, 128], P(('grp', 'tm'), ('mesh', 'rep')), parts along dimension 0
There are 2 independent parts, one for each index of `grp`. A program takes and returns all parts, laid end to end along the dimension named above; an argument that names none is the same for every part. Nothing has to cross between parts.
Inputs may be any that keep to these rules, and one draw needn't show every extreme that they name: face_counts[n(p, e), e'] = face_counts[p, e]; every partition sends 4 blocks toward at least one direction. `face_blocks`: the 4 blocks of one partition and direction are distinct. `near_columns`: for j < 3, slot 2j over the block rows of a partition is a permutation of its local blocks and slot 2j + 1 is the inverse permutation. `near_stiffness`: for j < 3, the block in slot 2j + 1 of block row b is the transpose of the block in slot 2j of the block row that slot 2j + 1 of b names. `far_stiffness`: G[n(p, e), e' * 4 + f] is the transpose of G[p, e * 4 + f].
All inputs are finite; a program needn't handle non-finite values.
Results may differ from a plain program's by a relative error of at most 0.00016.
Values sent between devices are 32-bit elements; how exact they have to be, the bound alone decides.
No kernel may reach another device: no remote copies, remote signals or barrier semaphores. Data moves between devices by JAX's collectives and lax.ppermute only.
A program may use at most 64 MiB of HBM per device.

v0:
```python
import jax
import jax.numpy as jnp
from jax import lax
from jax.sharding import PartitionSpec as P

ITERS = 2


def from_behind(block, axis, distance):
    devices = range(lax.axis_size(axis))
    route = [((i - distance) % len(devices), i) for i in devices]
    return lax.ppermute(block, axis, route)


def with_halo(value, sides, width):
    for axis, dim in sides:
        peers, length = (lax.axis_size(axis), value.shape[dim])
        up = [(i, (i + 1) % peers) for i in range(peers - 1)]
        down = [(j, i) for i, j in up]
        last = lax.slice_in_dim(value, length - width, length, axis=dim)
        initial = lax.slice_in_dim(value, 0, width, axis=dim)
        before = lax.ppermute(last, axis, up)
        after = lax.ppermute(initial, axis, down)
        value = jnp.concatenate([before, value, after], axis=dim)
    return value


def spatial(
    vector, kappa_sq, near_stiffness, far_stiffness, near_columns, face_blocks, face_counts
):
    hours_n, blocks_n, node_width, probes = vector.shape
    face_slots = face_blocks.shape[2]
    partitions = lax.axis_size(("mesh", "rep"))
    stride = partitions // 4 + 1
    offsets = (1, -1, 2, -2, stride, -stride)
    slot_blocks = face_blocks[0].reshape(-1)
    active = (jnp.arange(face_slots)[None, :] < face_counts[0][:, None]).astype(jnp.float32)
    outgoing = jnp.take(vector, slot_blocks, axis=1).reshape(
        hours_n, 6, face_slots, node_width, probes
    )
    outgoing = outgoing * active[None, :, :, None, None]
    arrived = []
    for heading in range(6):
        arrived.append(from_behind(outgoing[:, heading ^ 1], ("mesh", "rep"), -offsets[heading]))
    received = jnp.stack(arrived, axis=1).reshape(hours_n, 6 * face_slots, node_width, probes)
    nearby = jnp.take(vector, near_columns.reshape(-1), axis=1).reshape(
        hours_n, blocks_n, -1, probes
    )
    result = (3.0 + kappa_sq)[None, :, :, None] * vector
    result = result + jnp.einsum(
        "nik,hnkp->hnip",
        near_stiffness,
        nearby,
        precision=lax.Precision.HIGHEST,
        preferred_element_type=jnp.float32,
    )
    far_blocks = far_stiffness[0].reshape(node_width, 6 * face_slots, node_width)
    far_terms = jnp.einsum(
        "iqk,hqkp->hqip",
        far_blocks,
        received,
        precision=lax.Precision.HIGHEST,
        preferred_element_type=jnp.float32,
    )
    landing = (slot_blocks[None, :] == jnp.arange(blocks_n)[:, None]).astype(jnp.float32)
    result = result + jnp.einsum(
        "nq,hqip->hnip",
        landing,
        far_terms,
        precision=lax.Precision.HIGHEST,
        preferred_element_type=jnp.float32,
    )
    return result


def operate(
    vector,
    kappa_sq,
    time_coupling,
    near_stiffness,
    far_stiffness,
    near_columns,
    face_blocks,
    face_counts,
):
    product = spatial(
        vector, kappa_sq, near_stiffness, far_stiffness, near_columns, face_blocks, face_counts
    )
    padded = with_halo(product, (("tm", 0),), 1)
    return product - time_coupling[0] * (padded[:-2] + padded[2:])


def two_products(residual, applied):
    return lax.psum(
        (jnp.sum(residual * residual, axis=(0, 1, 2)), jnp.sum(residual * applied, axis=(0, 1, 2))),
        ("mesh", "tm", "rep"),
    )


def shards(
    right_side,
    kappa_sq,
    time_coupling,
    near_stiffness,
    far_stiffness,
    near_columns,
    face_blocks,
    face_counts,
):

    def apply_operator(vector):
        return operate(
            vector,
            kappa_sq,
            time_coupling,
            near_stiffness,
            far_stiffness,
            near_columns,
            face_blocks,
            face_counts,
        )

    solution_field = jnp.zeros_like(right_side)
    residual = right_side
    applied = apply_operator(residual)
    norm_now, product = two_products(residual, applied)
    step_size = norm_now / product
    direction = residual
    applied_dir = applied
    for iteration in range(ITERS):
        solution_field = solution_field + step_size * direction
        residual = residual - step_size * applied_dir
        if iteration + 1 < ITERS:
            applied = apply_operator(residual)
            norm_next, product = two_products(residual, applied)
            beta_ratio = norm_next / norm_now
            step_size = norm_next / (product - beta_ratio * norm_next / step_size)
            direction = residual + beta_ratio * direction
            applied_dir = applied + beta_ratio * applied_dir
            norm_now = norm_next
    return (solution_field, residual)


def solution(mesh):
    placed = (
        P(("grp", "tm"), ("mesh", "rep"), None, None),
        P(("grp", "mesh", "rep"), None),
        P("grp"),
        P(("mesh", "rep"), None, None),
        P(("mesh", "rep"), None, None),
        P(("mesh", "rep"), None),
        P(("mesh", "rep"), None, None),
        P(("mesh", "rep"), None),
    )
    return jax.shard_map(
        shards,
        mesh=mesh,
        in_specs=placed,
        out_specs=(
            P(("grp", "tm"), ("mesh", "rep"), None, None),
            P(("grp", "tm"), ("mesh", "rep"), None, None),
        ),
        check_vma=False,
    )
```

profile of v0, /device:TPU:0, one launch (start us, length us, event | category | flops | bytes accessed | tf_op | source)
XLA Modules:
  0.0 164.5 jit_solution(14381647301428617906)
XLA Ops:
  0.6 0.0 copy-start
  0.6 0.9 copy.19
  1.5 0.1 reshape_squeeze.8
  1.6 0.5 copy-done.8
  2.1 0.7 fusion.15
  2.9 0.8 copy.18
  3.6 0.1 reshape.135
  3.7 0.0 copy-start.4
  3.8 1.7 %gather_fusion.1 = f32[24,64,128]{2,1,0:T(8,128)S(1)} fusion(f32[16,64,128]{2,1,0:T(8,128)} %bitcast.116, s32[1024]{0:T(1024)S(1)} %get-tuple-element.30), kind=kCustom, calls=%fused_computation.1.clone | custom fusion | bytes 1572960 | tf_op jit(solution)/shard_map/jit(_take)/gather | solution.py:38
  5.5 0.0 copy-start.1
  5.5 0.1 bitcast_select_fusion.3
  5.6 0.1 broadcast_multiply_fusion.1
  5.7 0.8 slice_bitcast_fusion.6
  6.5 2.5 %collective-permute-start.5 = (f32[1,4,64,128]{3,2,1,0:T(8,128)S(1)}, f32[1,4,64,128]{3,2,1,0:T(8,128)}, u32[]{:S(2)}, u32[]{:S(2)}) collective-permute-start(f32[1,4,64,128]{3,2,1,0:T(8,128)S(1)} %get-tuple-element.22), channel_id=1, source_target_pairs={{9,0},{12,1},{13,4},{0,5},{1,8},{4,9},{5,12},{8,13},{11,2},{14,3},... | collective-permute-start | bytes 393224 | tf_op jit(solution)/shard_map/ppermute | solution.py:12
  9.0 1.0 collective-permute-start.4
  10.0 2.2 %collective-permute-start.3 = (f32[1,4,64,128]{3,2,1,0:T(8,128)}, f32[1,4,64,128]{3,2,1,0:T(8,128)}, u32[]{:S(2)}, u32[]{:S(2)}) collective-permute-start(f32[1,4,64,128]{3,2,1,0:T(8,128)} %get-tuple-element.24), channel_id=1, source_target_pairs={{12,0},{13,1},{0,4},{1,5},{4,8},{5,9},{8,12},{9,13},{14,2},{15,3},... | collective-permute-start | bytes 393224 | tf_op jit(solution)/shard_map/ppermute | solution.py:12
  12.2 2.0 %collective-permute-start.2 = (f32[1,4,64,128]{3,2,1,0:T(8,128)}, f32[1,4,64,128]{3,2,1,0:T(8,128)}, u32[]{:S(2)}, u32[]{:S(2)}) collective-permute-start(f32[1,4,64,128]{3,2,1,0:T(8,128)} %get-tuple-element.25), channel_id=1, source_target_pairs={{4,0},{5,1},{8,4},{9,5},{12,8},{13,9},{0,12},{1,13},{6,2},{7,3},{1... | collective-permute-start | bytes 393224 | tf_op jit(solution)/shard_map/ppermute | solution.py:12
  14.2 0.7 collective-permute-start
  14.9 0.2 reshape_squeeze.9
  15.1 2.4 %gather_fusion = f32[96,64,128]{2,1,0:T(8,128)} fusion(f32[16,64,128]{2,1,0:T(8,128)S(1)} %bitcast.117, s32[1024]{0:T(1024)S(1)} %get-tuple-element.31), kind=kCustom, calls=%fused_computation.clone | custom fusion | bytes 6291840 | tf_op jit(solution)/shard_map/jit(_take)/gather | solution.py:46
  17.5 2.2 %bitcast_select_fusion.1 = f32[1,96,64,128]{3,2,1,0:T(8,128)S(1)} fusion(f32[96,64,128]{2,1,0:T(8,128)} %gather_fusion, pred[96]{0:T(512)(128)(4,1)S(1)} %compare_and_fusion.1), kind=kLoop, calls=%fused_computation.5 | loop fusion | flops 786432 | bytes 6291552 | tf_op jit(solution)/shard_map/jit(_take)/select_n | solution.py:46
  19.7 3.2 %collective-permute-done = f32[1,4,64,128]{3,2,1,0:T(8,128)} collective-permute-done((f32[1,4,64,128]{3,2,1,0:T(8,128)}, f32[1,4,64,128]{3,2,1,0:T(8,128)}, u32[]{:S(2)}, u32[]{:S(2)}) %collective-permute-start) | collective-permute-done | bytes 131104 | tf_op jit(solution)/shard_map/ppermute | solution.py:12
  22.9 1.4 collective-permute-start.1
  24.3 0.9 bitcast_dynamic-update-slice_fusion.11
  25.2 4.2 %collective-permute-done.1 = f32[1,4,64,128]{3,2,1,0:T(8,128)S(1)} collective-permute-done((f32[1,4,64,128]{3,2,1,0:T(8,128)S(1)}, f32[1,4,64,128]{3,2,1,0:T(8,128)S(1)}, u32[]{:S(2)}, u32[]{:S(2)}) %collective-permute-start.1) | collective-permute-done | bytes 131104 | tf_op jit(solution)/shard_map/ppermute | solution.py:12
  29.4 0.9 bitcast_dynamic-update-slice_fusion.9
  30.3 0.0 collective-permute-done.3
  30.3 0.9 bitcast_dynamic-update-slice_fusion.8
  31.3 0.0 collective-permute-done.4
  31.3 0.9 bitcast_dynamic-update-slice_fusion.7
  32.2 0.9 bitcast_dynamic-update-slice_fusion.6
  33.1 0.9 convolution_bitcast_fusion.1
  34.1 0.9 fusion.6
  34.9 2.6 %fusion.1 = f32[1,16,64,128]{3,2,1,0:T(8,128)S(1)} fusion(f32[16,384,128]{2,1,0:T(8,128)S(1)} %bitcast.121, f32[16,64,384]{2,1,0:T(8,128)S(1)} %copy-done, f32[64,128,16]{1,2,0:T(8,128)S(1)} %fusion.6, f32[1,16,64,128]{3,2,1,0:T(8,128)S(1)} %copy-done.1, f32[16,64]{1,0:T(8,128)S(1)} %broadcast_add_fusion), kind=kOutput, calls=%fused_computation.11 | convolution fusion | flops 604372992 | bytes 6295552 | tf_op jit(solution)/shard_map/nik,hnkp->hnip/dot_general | solution.py:50
  37.5 1.3 collective-permute-start.7
  38.8 4.6 %collective-permute-start.6 = (f32[1,16,64,128]{3,2,1,0:T(8,128)S(1)}, f32[1,16,64,128]{3,2,1,0:T(8,128)S(1)}, u32[]{:S(2)}, u32[]{:S(2)}) collective-permute-start(f32[1,16,64,128]{3,2,1,0:T(8,128)S(1)} %fusion.1), channel_id=1, source_target_pairs={{0,2},{1,3},{4,6},{5,7},{8,10},{9,11},{12,14},{13,15},{16,18},{17,... | collective-permute-start | bytes 1572872 | tf_op jit(solution)/shard_map/ppermute | solution.py:22
  44.1 6.0 %collective-permute-done.7 = f32[1,16,64,128]{3,2,1,0:T(8,128)S(1)} collective-permute-done((f32[1,16,64,128]{3,2,1,0:T(8,128)S(1)}, f32[1,16,64,128]{3,2,1,0:T(8,128)S(1)}, u32[]{:S(2)}, u32[]{:S(2)}) %collective-permute-start.7) | collective-permute-done | bytes 524320 | tf_op jit(solution)/shard_map/ppermute | solution.py:23
  50.1 1.2 collective-permute-done.6
  51.3 1.0 multiply_reduce_fusion.2
  52.3 32.0 %all-reduce.1 = (f32[128]{0:T(128)S(1)}, f32[128]{0:T(128)S(1)}) all-reduce(f32[128]{0:T(128)S(1)} %get-tuple-element.7, f32[128]{0:T(128)S(1)} %get-tuple-element.6), channel_id=1, replica_groups=mesh['grp'=2,'mesh'=4,'tm'=2,'rep'=2] {'mesh','tm','rep'}, use_global_device_ids=true, to_apply=%region_1.2 | all-reduce | flops 256 | bytes 2048 | tf_op jit(solution)/shard_map/psum | solution.py:94
  84.2 1.1 multiply_subtract_fusion.2
  85.3 1.6 gather_fusion.3
  87.0 2.4 %gather_fusion.2 = f32[96,64,128]{2,1,0:T(8,128)} fusion(f32[16,64,128]{2,1,0:T(8,128)S(1)} %bitcast.119, s32[1024]{0:T(1024)S(1)} %get-tuple-element.31), kind=kCustom, calls=%fused_computation.2.clone | custom fusion | bytes 6291840 | tf_op jit(solution)/shard_map/jit(_take)/gather | solution.py:46
  89.4 1.4 bitcast_select_fusion.2
  90.8 0.1 broadcast_multiply_fusion
  90.9 0.1 slice_bitcast_fusion
  91.0 0.1 collective-permute-start.13
  91.0 2.6 %collective-permute-start.12 = (f32[1,4,64,128]{3,2,1,0:T(8,128)S(1)}, f32[1,4,64,128]{3,2,1,0:T(8,128)S(1)}, u32[]{:S(2)}, u32[]{:S(2)}) collective-permute-start(f32[1,4,64,128]{3,2,1,0:T(8,128)S(1)} %get-tuple-element.17), channel_id=1, source_target_pairs={{5,0},{8,1},{9,4},{12,5},{13,8},{0,9},{1,12},{4,13},{7,2},{10,3},{... | collective-permute-start | bytes 393224 | tf_op jit(solution)/shard_map/ppermute | solution.py:12
  93.7 3.8 %collective-permute-start.10 = (f32[1,4,64,128]{3,2,1,0:T(8,128)S(1)}, f32[1,4,64,128]{3,2,1,0:T(8,128)S(1)}, u32[]{:S(2)}, u32[]{:S(2)}) collective-permute-start(f32[1,4,64,128]{3,2,1,0:T(8,128)S(1)} %get-tuple-element.19), channel_id=1, source_target_pairs={{4,0},{5,1},{8,4},{9,5},{12,8},{13,9},{0,12},{1,13},{6,2},{7,3},{1... | collective-permute-start | bytes 393224 | tf_op jit(solution)/shard_map/ppermute | solution.py:12
  97.5 0.3 bitcast_select_fusion
  97.8 5.5 %collective-permute-done.8 = f32[1,4,64,128]{3,2,1,0:T(8,128)S(1)} collective-permute-done((f32[1,4,64,128]{3,2,1,0:T(8,128)S(1)}, f32[1,4,64,128]{3,2,1,0:T(8,128)S(1)}, u32[]{:S(2)}, u32[]{:S(2)}) %collective-permute-start.8) | collective-permute-done | bytes 131104 | tf_op jit(solution)/shard_map/ppermute | solution.py:12
  103.3 2.1 %collective-permute-start.9 = (f32[1,4,64,128]{3,2,1,0:T(8,128)S(1)}, f32[1,4,64,128]{3,2,1,0:T(8,128)S(1)}, u32[]{:S(2)}, u32[]{:S(2)}) collective-permute-start(f32[1,4,64,128]{3,2,1,0:T(8,128)S(1)} %get-tuple-element.20), channel_id=1, source_target_pairs={{13,0},{0,1},{1,4},{4,5},{5,8},{8,9},{9,12},{12,13},{15,2},{2,3},{... | collective-permute-start | bytes 393224 | tf_op jit(solution)/shard_map/ppermute | solution.py:12
  105.5 4.3 %collective-permute-done.9 = f32[1,4,64,128]{3,2,1,0:T(8,128)S(1)} collective-permute-done((f32[1,4,64,128]{3,2,1,0:T(8,128)S(1)}, f32[1,4,64,128]{3,2,1,0:T(8,128)S(1)}, u32[]{:S(2)}, u32[]{:S(2)}) %collective-permute-start.9) | collective-permute-done | bytes 131104 | tf_op jit(solution)/shard_map/ppermute | solution.py:12
  109.9 0.9 convolution_bitcast_fusion
  110.9 0.9 fusion.4
  111.7 0.0 copy-start.3
  111.8 2.6 %fusion.3 = f32[1,16,64,128]{3,2,1,0:T(8,128)S(1)} fusion(f32[16,384,128]{2,1,0:T(8,128)S(1)} %bitcast.120, f32[16,64,384]{2,1,0:T(8,128)S(1)} %copy-done, f32[64,128,16]{1,2,0:T(8,128)S(1)} %fusion.4, f32[1,16,64,128]{3,2,1,0:T(8,128)S(1)} %multiply_subtract_fusion.2, f32[16,64]{1,0:T(8,128)S(1)} %broadcast_add_fusion), kind=kOutput, calls=%fused_computation.13 | convolution fusion | flops 604372992 | bytes 6295552 | tf_op jit(solution)/shard_map/nik,hnkp->hnip/dot_general | solution.py:50
  114.4 1.3 collective-permute-start.15
  115.7 4.6 %collective-permute-start.14 = (f32[1,16,64,128]{3,2,1,0:T(8,128)S(1)}, f32[1,16,64,128]{3,2,1,0:T(8,128)S(1)}, u32[]{:S(2)}, u32[]{:S(2)}) collective-permute-start(f32[1,16,64,128]{3,2,1,0:T(8,128)S(1)} %fusion.3), channel_id=1, source_target_pairs={{0,2},{1,3},{4,6},{5,7},{8,10},{9,11},{12,14},{13,15},{16,18},{17,... | collective-permute-start | bytes 1572872 | tf_op jit(solution)/shard_map/ppermute | solution.py:22
  120.3 7.4 %collective-permute-done.15 = f32[1,16,64,128]{3,2,1,0:T(8,128)S(1)} collective-permute-done((f32[1,16,64,128]{3,2,1,0:T(8,128)S(1)}, f32[1,16,64,128]{3,2,1,0:T(8,128)S(1)}, u32[]{:S(2)}, u32[]{:S(2)}) %collective-permute-start.15) | collective-permute-done | bytes 524320 | tf_op jit(solution)/shard_map/ppermute | solution.py:23
  127.7 1.2 collective-permute-done.14
  128.9 1.0 multiply_reduce_fusion
  129.9 32.4 %all-reduce = (f32[128]{0:T(128)S(1)}, f32[128]{0:T(128)S(1)}) all-reduce(f32[128]{0:T(128)S(1)} %get-tuple-element.5, f32[128]{0:T(128)S(1)} %get-tuple-element.4), channel_id=1, replica_groups=mesh['grp'=2,'mesh'=4,'tm'=2,'rep'=2] {'mesh','tm','rep'}, use_global_device_ids=true, to_apply=%region_5.8 | all-reduce | flops 256 | bytes 2048 | tf_op jit(solution)/shard_map/psum | solution.py:94
  162.3 2.2 %multiply_subtract_fusion = (f32[1,16,64,128]{3,2,1,0:T(8,128)}, f32[1,16,64,128]{3,2,1,0:T(8,128)}) fusion(f32[1,16,64,128]{3,2,1,0:T(8,128)S(1)} %multiply_subtract_fusion.2, f32[1,16,64,128]{3,2,1,0:T(8,128)} %get-tuple-element.14, f32[1,16,64,128]{3,2,1,0:T(8,128)S(1)} %copy-done.3, f32[128]{0:T(128)S(1)} %get-tuple-element.13, ...), kind=kLoop, calls=%fused_computation.22 | loop fusion | flops 1179648 | bytes 3147264 | tf_op jit(solution)/shard_map/sub | solution.py:132
  (48 shorter events, 0.2 us)
Async XLA Ops:
  0.6 34.3 %copy-start = (f32[16,64,384]{2,1,0:T(8,128)S(1)}, f32[16,64,384]{2,1,0:T(8,128)}, u32[]{:S(2)}) copy-start(f32[16,64,384]{2,1,0:T(8,128)} %param.15) | copy-start | bytes 4718596
  1.6 0.5 copy-start.8
  1.6 4.0 %copy-start.11 = (pred[24]{0:T(512)(128)(4,1)}, pred[24]{0:T(512)(128)(4,1)S(1)}, u32[]{:S(2)}) copy-start(pred[24]{0:T(512)(128)(4,1)S(1)} %compare_and_fusion) | copy-start | bytes 76
  3.7 1.9 %copy-start.7 = (s32[1024]{0:T(1024)}, s32[1024]{0:T(1024)S(1)}, u32[]{:S(2)}) copy-start(s32[1024]{0:T(1024)S(1)} %get-tuple-element.30) | copy-start | bytes 12292
  3.7 11.2 %copy-start.4 = (f32[1,64,1536]{2,1,0:T(8,128)S(1)}, f32[1,64,1536]{2,1,0:T(8,128)}, u32[]{:S(2)}) copy-start(f32[1,64,1536]{2,1,0:T(8,128)} %param.16) | copy-start | bytes 1179652
  5.5 9.6 %copy-start.1 = (f32[1,16,64,128]{3,2,1,0:T(8,128)S(1)}, f32[1,16,64,128]{3,2,1,0:T(8,128)}, u32[]{:S(2)}) copy-start(f32[1,16,64,128]{3,2,1,0:T(8,128)} %param.12) | copy-start | bytes 1572868
  6.5 25.7 %collective-permute-start.5 = (f32[1,4,64,128]{3,2,1,0:T(8,128)S(1)}, f32[1,4,64,128]{3,2,1,0:T(8,128)}, u32[]{:S(2)}, u32[]{:S(2)}) collective-permute-start(f32[1,4,64,128]{3,2,1,0:T(8,128)S(1)} %get-tuple-element.22), channel_id=1, source_target_pairs={{9,0},{12,1},{13,4},{0,5},{1,8},{4,9},{5,12},{8,13},{11,2},{14,3},... | collective-permute-start | bytes 393224 | tf_op jit(solution)/shard_map/ppermute | solution.py:12
  9.0 22.3 %collective-permute-start.4 = (f32[1,4,64,128]{3,2,1,0:T(8,128)S(1)}, f32[1,4,64,128]{3,2,1,0:T(8,128)}, u32[]{:S(2)}, u32[]{:S(2)}) collective-permute-start(f32[1,4,64,128]{3,2,1,0:T(8,128)S(1)} %get-tuple-element.23), channel_id=1, source_target_pairs={{5,0},{8,1},{9,4},{12,5},{13,8},{0,9},{1,12},{4,13},{7,2},{10,3},{... | collective-permute-start | bytes 393224 | tf_op jit(solution)/shard_map/ppermute | solution.py:12
  10.0 20.3 %collective-permute-start.3 = (f32[1,4,64,128]{3,2,1,0:T(8,128)}, f32[1,4,64,128]{3,2,1,0:T(8,128)}, u32[]{:S(2)}, u32[]{:S(2)}) collective-permute-start(f32[1,4,64,128]{3,2,1,0:T(8,128)} %get-tuple-element.24), channel_id=1, source_target_pairs={{12,0},{13,1},{0,4},{1,5},{4,8},{5,9},{8,12},{9,13},{14,2},{15,3},... | collective-permute-start | bytes 393224 | tf_op jit(solution)/shard_map/ppermute | solution.py:12
  12.2 17.2 %collective-permute-start.2 = (f32[1,4,64,128]{3,2,1,0:T(8,128)}, f32[1,4,64,128]{3,2,1,0:T(8,128)}, u32[]{:S(2)}, u32[]{:S(2)}) collective-permute-start(f32[1,4,64,128]{3,2,1,0:T(8,128)} %get-tuple-element.25), channel_id=1, source_target_pairs={{4,0},{5,1},{8,4},{9,5},{12,8},{13,9},{0,12},{1,13},{6,2},{7,3},{1... | collective-permute-start | bytes 393224 | tf_op jit(solution)/shard_map/ppermute | solution.py:12
  14.2 8.7 %collective-permute-start = (f32[1,4,64,128]{3,2,1,0:T(8,128)}, f32[1,4,64,128]{3,2,1,0:T(8,128)}, u32[]{:S(2)}, u32[]{:S(2)}) collective-permute-start(f32[1,4,64,128]{3,2,1,0:T(8,128)} %get-tuple-element.27), channel_id=1, source_target_pairs={{1,0},{4,1},{5,4},{8,5},{9,8},{12,9},{13,12},{0,13},{3,2},{6,3},{7... | collective-permute-start | bytes 393224 | tf_op jit(solution)/shard_map/ppermute | solution.py:12
  14.9 2.6 %copy-start.13 = (pred[96]{0:T(512)(128)(4,1)}, pred[96]{0:T(512)(128)(4,1)S(1)}, u32[]{:S(2)}) copy-start(pred[96]{0:T(512)(128)(4,1)S(1)} %compare_and_fusion.1) | copy-start | bytes 292
  17.5 2.2 %copy-start.6 = (f32[16,64]{1,0:T(8,128)S(1)}, f32[16,64]{1,0:T(8,128)}, u32[]{:S(2)}) copy-start(f32[16,64]{1,0:T(8,128)} %param.13) | copy-start | bytes 12292
  17.5 5.4 %copy-start.5 = (f32[1,4,64,128]{3,2,1,0:T(8,128)S(1)}, f32[1,4,64,128]{3,2,1,0:T(8,128)}, u32[]{:S(2)}) copy-start(f32[1,4,64,128]{3,2,1,0:T(8,128)} %get-tuple-element.26) | copy-start | bytes 393220
  19.7 14.3 %copy-start.9 = (s32[24]{0:T(128)S(1)}, s32[24]{0:T(128)}, u32[]{:S(2)}) copy-start(s32[24]{0:T(128)} %copy-done.8) | copy-start | bytes 292
  22.9 6.5 %collective-permute-start.1 = (f32[1,4,64,128]{3,2,1,0:T(8,128)S(1)}, f32[1,4,64,128]{3,2,1,0:T(8,128)S(1)}, u32[]{:S(2)}, u32[]{:S(2)}) collective-permute-start(f32[1,4,64,128]{3,2,1,0:T(8,128)S(1)} %copy-done.5), channel_id=1, source_target_pairs={{13,0},{0,1},{1,4},{4,5},{5,8},{8,9},{9,12},{12,13},{15,2},{2,3},{... | collective-permute-start | bytes 393224 | tf_op jit(solution)/shard_map/ppermute | solution.py:12
  37.5 12.6 %collective-permute-start.7 = (f32[1,16,64,128]{3,2,1,0:T(8,128)S(1)}, f32[1,16,64,128]{3,2,1,0:T(8,128)S(1)}, u32[]{:S(2)}, u32[]{:S(2)}) collective-permute-start(f32[1,16,64,128]{3,2,1,0:T(8,128)S(1)} %fusion.1), channel_id=1, source_target_pairs={{2,0},{3,1},{6,4},{7,5},{10,8},{11,9},{14,12},{15,13},{18,16},{19,... | collective-permute-start | bytes 1572872 | tf_op jit(solution)/shard_map/ppermute | solution.py:23
  38.8 12.5 %collective-permute-start.6 = (f32[1,16,64,128]{3,2,1,0:T(8,128)S(1)}, f32[1,16,64,128]{3,2,1,0:T(8,128)S(1)}, u32[]{:S(2)}, u32[]{:S(2)}) collective-permute-start(f32[1,16,64,128]{3,2,1,0:T(8,128)S(1)} %fusion.1), channel_id=1, source_target_pairs={{0,2},{1,3},{4,6},{5,7},{8,10},{9,11},{12,14},{13,15},{16,18},{17,... | collective-permute-start | bytes 1572872 | tf_op jit(solution)/shard_map/ppermute | solution.py:22
  87.0 2.4 %copy-start.12 = (pred[24]{0:T(512)(128)(4,1)S(1)}, pred[24]{0:T(512)(128)(4,1)}, u32[]{:S(2)}) copy-start(pred[24]{0:T(512)(128)(4,1)} %copy-done.11) | copy-start | bytes 76
  89.4 8.1 %copy-start.2 = (f32[96,64,128]{2,1,0:T(8,128)S(1)}, f32[96,64,128]{2,1,0:T(8,128)}, u32[]{:S(2)}) copy-start(f32[96,64,128]{2,1,0:T(8,128)} %gather_fusion.2) | copy-start | bytes 9437188
  89.4 8.1 %copy-start.14 = (pred[96]{0:T(512)(128)(4,1)S(1)}, pred[96]{0:T(512)(128)(4,1)}, u32[]{:S(2)}) copy-start(pred[96]{0:T(512)(128)(4,1)} %copy-done.13) | copy-start | bytes 292
  91.0 18.9 %collective-permute-start.13 = (f32[1,4,64,128]{3,2,1,0:T(8,128)S(1)}, f32[1,4,64,128]{3,2,1,0:T(8,128)S(1)}, u32[]{:S(2)}, u32[]{:S(2)}) collective-permute-start(f32[1,4,64,128]{3,2,1,0:T(8,128)S(1)} %get-tuple-element.16), channel_id=1, source_target_pairs={{9,0},{12,1},{13,4},{0,5},{1,8},{4,9},{5,12},{8,13},{11,2},{14,3},... | collective-permute-start | bytes 393224 | tf_op jit(solution)/shard_map/ppermute | solution.py:12
  91.0 18.8 %collective-permute-start.12 = (f32[1,4,64,128]{3,2,1,0:T(8,128)S(1)}, f32[1,4,64,128]{3,2,1,0:T(8,128)S(1)}, u32[]{:S(2)}, u32[]{:S(2)}) collective-permute-start(f32[1,4,64,128]{3,2,1,0:T(8,128)S(1)} %get-tuple-element.17), channel_id=1, source_target_pairs={{5,0},{8,1},{9,4},{12,5},{13,8},{0,9},{1,12},{4,13},{7,2},{10,3},{... | collective-permute-start | bytes 393224 | tf_op jit(solution)/shard_map/ppermute | solution.py:12
  93.7 16.2 %collective-permute-start.11 = (f32[1,4,64,128]{3,2,1,0:T(8,128)S(1)}, f32[1,4,64,128]{3,2,1,0:T(8,128)S(1)}, u32[]{:S(2)}, u32[]{:S(2)}) collective-permute-start(f32[1,4,64,128]{3,2,1,0:T(8,128)S(1)} %get-tuple-element.18), channel_id=1, source_target_pairs={{12,0},{13,1},{0,4},{1,5},{4,8},{5,9},{8,12},{9,13},{14,2},{15,3},... | collective-permute-start | bytes 393224 | tf_op jit(solution)/shard_map/ppermute | solution.py:12
  93.7 16.2 %collective-permute-start.10 = (f32[1,4,64,128]{3,2,1,0:T(8,128)S(1)}, f32[1,4,64,128]{3,2,1,0:T(8,128)S(1)}, u32[]{:S(2)}, u32[]{:S(2)}) collective-permute-start(f32[1,4,64,128]{3,2,1,0:T(8,128)S(1)} %get-tuple-element.19), channel_id=1, source_target_pairs={{4,0},{5,1},{8,4},{9,5},{12,8},{13,9},{0,12},{1,13},{6,2},{7,3},{1... | collective-permute-start | bytes 393224 | tf_op jit(solution)/shard_map/ppermute | solution.py:12
  97.5 5.9 %collective-permute-start.8 = (f32[1,4,64,128]{3,2,1,0:T(8,128)S(1)}, f32[1,4,64,128]{3,2,1,0:T(8,128)S(1)}, u32[]{:S(2)}, u32[]{:S(2)}) collective-permute-start(f32[1,4,64,128]{3,2,1,0:T(8,128)S(1)} %get-tuple-element.21), channel_id=1, source_target_pairs={{1,0},{4,1},{5,4},{8,5},{9,8},{12,9},{13,12},{0,13},{3,2},{6,3},{7... | collective-permute-start | bytes 393224 | tf_op jit(solution)/shard_map/ppermute | solution.py:12
  97.8 13.1 %copy-start.10 = (s32[24]{0:T(128)S(1)}, s32[24]{0:T(128)}, u32[]{:S(2)}) copy-start(s32[24]{0:T(128)} %copy-done.8) | copy-start | bytes 292
  103.3 6.5 %collective-permute-start.9 = (f32[1,4,64,128]{3,2,1,0:T(8,128)S(1)}, f32[1,4,64,128]{3,2,1,0:T(8,128)S(1)}, u32[]{:S(2)}, u32[]{:S(2)}) collective-permute-start(f32[1,4,64,128]{3,2,1,0:T(8,128)S(1)} %get-tuple-element.20), channel_id=1, source_target_pairs={{13,0},{0,1},{1,4},{4,5},{5,8},{8,9},{9,12},{12,13},{15,2},{2,3},{... | collective-permute-start | bytes 393224 | tf_op jit(solution)/shard_map/ppermute | solution.py:12
  111.7 50.6 %copy-start.3 = (f32[1,16,64,128]{3,2,1,0:T(8,128)S(1)}, f32[1,16,64,128]{3,2,1,0:T(8,128)}, u32[]{:S(2)}) copy-start(f32[1,16,64,128]{3,2,1,0:T(8,128)} %get-tuple-element.15) | copy-start | bytes 1572868
  114.4 13.3 %collective-permute-start.15 = (f32[1,16,64,128]{3,2,1,0:T(8,128)S(1)}, f32[1,16,64,128]{3,2,1,0:T(8,128)S(1)}, u32[]{:S(2)}, u32[]{:S(2)}) collective-permute-start(f32[1,16,64,128]{3,2,1,0:T(8,128)S(1)} %fusion.3), channel_id=1, source_target_pairs={{2,0},{3,1},{6,4},{7,5},{10,8},{11,9},{14,12},{15,13},{18,16},{19,... | collective-permute-start | bytes 1572872 | tf_op jit(solution)/shard_map/ppermute | solution.py:23
  115.7 13.2 %collective-permute-start.14 = (f32[1,16,64,128]{3,2,1,0:T(8,128)S(1)}, f32[1,16,64,128]{3,2,1,0:T(8,128)S(1)}, u32[]{:S(2)}, u32[]{:S(2)}) collective-permute-start(f32[1,16,64,128]{3,2,1,0:T(8,128)S(1)} %fusion.3), channel_id=1, source_target_pairs={{0,2},{1,3},{4,6},{5,7},{8,10},{9,11},{12,14},{13,15},{16,18},{17,... | collective-permute-start | bytes 1572872 | tf_op jit(solution)/shard_map/ppermute | solution.py:22
where the time goes:
time: 165 us
  blocking collectives  64.4 us (39%)
  waiting for transfers between devices  33.1 us (20%)
  starting transfers between devices  30.1 us (18%)
  local copies, waits for them, and re-layouts  16.1 us (10%)
  other arithmetic  10.3 us (6%)
  matrix products  8.76 us (5%)
  between operations  1.73 us (1%)
    psum x2, blocking collectives, two_products(): lax.psum((jnp.sum(residual * residual, axis=(0, 1, 2)), jnp.sum(residual...  64.4 us
    ppermute x12, starting transfers between devices, from_behind(): return lax.ppermute(block, axis, route)  18.3 us
    ppermute x12, waiting for transfers between devices, from_behind(): return lax.ppermute(block, axis, route)  17.3 us
    ppermute x2, waiting for transfers between devices, with_halo(): after = lax.ppermute(initial, axis, down)  13.4 us
    ppermute x2, starting transfers between devices, with_halo(): before = lax.ppermute(last, axis, up)  9.21 us
    unnamed x42, local copies, waits for them, and re-layouts  5.93 us
    dot_general x2, matrix products, spatial(): jnp.einsum('nik,hnkp->hnip', near_stiffness, nearby, precision=lax.Precis...  5.2 us
    gather x2, local copies, waits for them, and re-layouts, spatial(): jnp.take(vector, near_columns.reshape(-1), axis=1)  4.79 us
  transfers between devices with their start and end apart: 16, of which 8 were waited for; matrix products, arithmetic and copies ran while one was open for 5% of the time, Pallas kernels for 0%

commit v1 on v0

--- a/solution.py
+++ b/solution.py
@@ -1,9 +1,18 @@
+import functools
 import jax
 import jax.numpy as jnp
 from jax import lax
 from jax.sharding import PartitionSpec as P
 
 ITERS = 2
+
+
+def lay_map(field, net_axis, peer_axis):
+    piece_next = lax.psum(lax.psum(field, net_axis), peer_axis)
+    return piece_next
+
+
+change_the_domain = functools.partial(lay_map, net_axis=("tm", "rep"), peer_axis="mesh")
 
 
 def from_behind(block, axis, distance):
@@ -91,9 +100,8 @@
 
 
 def two_products(residual, applied):
-    return lax.psum(
-        (jnp.sum(residual * residual, axis=(0, 1, 2)), jnp.sum(residual * applied, axis=(0, 1, 2))),
-        ("mesh", "tm", "rep"),
+    return change_the_domain(
+        (jnp.sum(residual * residual, axis=(0, 1, 2)), jnp.sum(residual * applied, axis=(0, 1, 2)))
     )
 
 

time: 165 us -> 138 us (0.84)
  blocking collectives: 64.4 us -> 37.3 us
    psum x2 -> x4, blocking collectives: 64.4 us -> 37.3 us  [lay_map(): piece_next = lax.psum(lax.psum(field, net_axis), peer_axis)]
  transfers between devices with their start and end apart: 16 -> 16, of which waited for: 8 -> 8; matrix products, arithmetic and copies ran while one was open for 5% -> 6% of each run, Pallas kernels for 0% -> 0%
where the time goes in v1:
time: 138 us
  blocking collectives  37.3 us (27%)
  waiting for transfers between devices  33.6 us (24%)
  starting transfers between devices  29.9 us (22%)
  local copies, waits for them, and re-layouts  16.2 us (12%)
  other arithmetic  10.3 us (7%)
  matrix products  8.77 us (6%)
  between operations  1.73 us (1%)
    psum x4, blocking collectives, lay_map(): piece_next = lax.psum(lax.psum(field, net_axis), peer_axis)  37.3 us
    ppermute x12, starting transfers between devices, from_behind(): return lax.ppermute(block, axis, route)  18.1 us
    ppermute x12, waiting for transfers between devices, from_behind(): return lax.ppermute(block, axis, route)  18 us
    ppermute x2, waiting for transfers between devices, with_halo(): after = lax.ppermute(initial, axis, down)  13.2 us
    ppermute x2, starting transfers between devices, with_halo(): before = lax.ppermute(last, axis, up)  9.21 us
    unnamed x42, local copies, waits for them, and re-layouts  5.93 us
    dot_general x2, matrix products, spatial(): jnp.einsum('nik,hnkp->hnip', near_stiffness, nearby, precision=lax.Precis...  5.2 us
    gather x2, local copies, waits for them, and re-layouts, spatial(): jnp.take(vector, near_columns.reshape(-1), axis=1)  4.79 us
  transfers between devices with their start and end apart: 16, of which 8 were waited for; matrix products, arithmetic and copies ran while one was open for 6% of the time, Pallas kernels for 0%

profile of v1, /device:TPU:0, one launch (start us, length us, event | category | flops | bytes accessed | tf_op | source)
XLA Modules:
  0.0 137.7 jit_solution(15012892423534685494)
XLA Ops:
  0.6 0.0 copy-start
  0.6 0.9 copy.19
  1.5 0.1 reshape_squeeze.8
  1.6 0.5 copy-done.8
  2.1 0.7 fusion.15
  2.9 0.8 copy.18
  3.6 0.1 reshape.135
  3.7 0.0 copy-start.4
  3.8 1.7 %gather_fusion.1 = f32[24,64,128]{2,1,0:T(8,128)S(1)} fusion(f32[16,64,128]{2,1,0:T(8,128)} %bitcast.116, s32[1024]{0:T(1024)S(1)} %get-tuple-element.34), kind=kCustom, calls=%fused_computation.1.clone | custom fusion | bytes 1572960 | tf_op jit(solution)/shard_map/jit(_take)/gather | solution.py:47
  5.5 0.0 copy-start.1
  5.5 0.1 bitcast_select_fusion.3
  5.6 0.1 broadcast_multiply_fusion.1
  5.7 0.8 slice_bitcast_fusion.6
  6.5 2.5 %collective-permute-start.5 = (f32[1,4,64,128]{3,2,1,0:T(8,128)S(1)}, f32[1,4,64,128]{3,2,1,0:T(8,128)}, u32[]{:S(2)}, u32[]{:S(2)}) collective-permute-start(f32[1,4,64,128]{3,2,1,0:T(8,128)S(1)} %get-tuple-element.26), channel_id=1, source_target_pairs={{9,0},{12,1},{13,4},{0,5},{1,8},{4,9},{5,12},{8,13},{11,2},{14,3},... | collective-permute-start | bytes 393224 | tf_op jit(solution)/shard_map/ppermute | solution.py:21
  9.0 1.0 collective-permute-start.4
  10.0 2.2 %collective-permute-start.3 = (f32[1,4,64,128]{3,2,1,0:T(8,128)}, f32[1,4,64,128]{3,2,1,0:T(8,128)}, u32[]{:S(2)}, u32[]{:S(2)}) collective-permute-start(f32[1,4,64,128]{3,2,1,0:T(8,128)} %get-tuple-element.28), channel_id=1, source_target_pairs={{12,0},{13,1},{0,4},{1,5},{4,8},{5,9},{8,12},{9,13},{14,2},{15,3},... | collective-permute-start | bytes 393224 | tf_op jit(solution)/shard_map/ppermute | solution.py:21
  12.2 2.0 %collective-permute-start.2 = (f32[1,4,64,128]{3,2,1,0:T(8,128)}, f32[1,4,64,128]{3,2,1,0:T(8,128)}, u32[]{:S(2)}, u32[]{:S(2)}) collective-permute-start(f32[1,4,64,128]{3,2,1,0:T(8,128)} %get-tuple-element.29), channel_id=1, source_target_pairs={{4,0},{5,1},{8,4},{9,5},{12,8},{13,9},{0,12},{1,13},{6,2},{7,3},{1... | collective-permute-start | bytes 393224 | tf_op jit(solution)/shard_map/ppermute | solution.py:21
  14.2 0.7 collective-permute-start
  14.9 0.2 reshape_squeeze.9
  15.1 2.4 %gather_fusion = f32[96,64,128]{2,1,0:T(8,128)} fusion(f32[16,64,128]{2,1,0:T(8,128)S(1)} %bitcast.117, s32[1024]{0:T(1024)S(1)} %get-tuple-element.35), kind=kCustom, calls=%fused_computation.clone | custom fusion | bytes 6291840 | tf_op jit(solution)/shard_map/jit(_take)/gather | solution.py:55
  17.5 2.2 %bitcast_select_fusion.1 = f32[1,96,64,128]{3,2,1,0:T(8,128)S(1)} fusion(f32[96,64,128]{2,1,0:T(8,128)} %gather_fusion, pred[96]{0:T(512)(128)(4,1)S(1)} %compare_and_fusion.1), kind=kLoop, calls=%fused_computation.5 | loop fusion | flops 786432 | bytes 6291552 | tf_op jit(solution)/shard_map/jit(_take)/select_n | solution.py:55
  19.8 3.2 %collective-permute-done = f32[1,4,64,128]{3,2,1,0:T(8,128)} collective-permute-done((f32[1,4,64,128]{3,2,1,0:T(8,128)}, f32[1,4,64,128]{3,2,1,0:T(8,128)}, u32[]{:S(2)}, u32[]{:S(2)}) %collective-permute-start) | collective-permute-done | bytes 131104 | tf_op jit(solution)/shard_map/ppermute | solution.py:21
  22.9 1.4 collective-permute-start.1
  24.3 0.9 bitcast_dynamic-update-slice_fusion.11
  25.2 4.2 %collective-permute-done.1 = f32[1,4,64,128]{3,2,1,0:T(8,128)S(1)} collective-permute-done((f32[1,4,64,128]{3,2,1,0:T(8,128)S(1)}, f32[1,4,64,128]{3,2,1,0:T(8,128)S(1)}, u32[]{:S(2)}, u32[]{:S(2)}) %collective-permute-start.1) | collective-permute-done | bytes 131104 | tf_op jit(solution)/shard_map/ppermute | solution.py:21
  29.4 0.9 bitcast_dynamic-update-slice_fusion.9
  30.4 0.9 bitcast_dynamic-update-slice_fusion.8
  31.3 0.9 bitcast_dynamic-update-slice_fusion.7
  32.2 0.9 bitcast_dynamic-update-slice_fusion.6
  33.1 0.9 convolution_bitcast_fusion.1
  34.1 0.9 fusion.6
  34.9 2.6 %fusion.1 = f32[1,16,64,128]{3,2,1,0:T(8,128)S(1)} fusion(f32[16,384,128]{2,1,0:T(8,128)S(1)} %bitcast.121, f32[16,64,384]{2,1,0:T(8,128)S(1)} %copy-done, f32[64,128,16]{1,2,0:T(8,128)S(1)} %fusion.6, f32[1,16,64,128]{3,2,1,0:T(8,128)S(1)} %copy-done.1, f32[16,64]{1,0:T(8,128)S(1)} %broadcast_add_fusion), kind=kOutput, calls=%fused_computation.11 | convolution fusion | flops 604372992 | bytes 6295552 | tf_op jit(solution)/shard_map/nik,hnkp->hnip/dot_general | solution.py:59
  37.5 1.3 collective-permute-start.7
  38.8 4.6 %collective-permute-start.6 = (f32[1,16,64,128]{3,2,1,0:T(8,128)S(1)}, f32[1,16,64,128]{3,2,1,0:T(8,128)S(1)}, u32[]{:S(2)}, u32[]{:S(2)}) collective-permute-start(f32[1,16,64,128]{3,2,1,0:T(8,128)S(1)} %fusion.1), channel_id=1, source_target_pairs={{0,2},{1,3},{4,6},{5,7},{8,10},{9,11},{12,14},{13,15},{16,18},{17,... | collective-permute-start | bytes 1572872 | tf_op jit(solution)/shard_map/ppermute | solution.py:31
  44.1 6.0 %collective-permute-done.7 = f32[1,16,64,128]{3,2,1,0:T(8,128)S(1)} collective-permute-done((f32[1,16,64,128]{3,2,1,0:T(8,128)S(1)}, f32[1,16,64,128]{3,2,1,0:T(8,128)S(1)}, u32[]{:S(2)}, u32[]{:S(2)}) %collective-permute-start.7) | collective-permute-done | bytes 524320 | tf_op jit(solution)/shard_map/ppermute | solution.py:32
  50.1 1.2 collective-permute-done.6
  51.3 1.0 multiply_reduce_fusion.2
  52.3 6.0 %all-reduce.1 = (f32[128]{0:T(128)S(1)}, f32[128]{0:T(128)S(1)}) all-reduce(f32[128]{0:T(128)S(1)} %get-tuple-element.7, f32[128]{0:T(128)S(1)} %get-tuple-element.6), channel_id=1, replica_groups=mesh['grp'=2,'mesh'=4,'tm'=2,'rep'=2] {'tm','rep'}, use_global_device_ids=true, to_apply=%region_1.2 | all-reduce | flops 256 | bytes 2048 | tf_op jit(solution)/shard_map/psum | solution.py:11
  58.3 13.5 %all-reduce.3 = (f32[128]{0:T(128)S(1)}, f32[128]{0:T(128)S(1)}) all-reduce(f32[128]{0:T(128)S(1)} %get-tuple-element.10, f32[128]{0:T(128)S(1)} %get-tuple-element.11), channel_id=1, replica_groups=mesh['grp'=2,'mesh'=4,'tm'=2,'rep'=2] {'mesh'}, use_global_device_ids=true, to_apply=%region_2.3 | all-reduce | flops 256 | bytes 2048 | tf_op jit(solution)/shard_map/psum | solution.py:11
  71.8 1.1 multiply_subtract_fusion.2
  72.9 1.6 %gather_fusion.3 = f32[24,64,128]{2,1,0:T(8,128)} fusion(f32[16,64,128]{2,1,0:T(8,128)S(1)} %bitcast.118, s32[1024]{0:T(1024)} %copy-done.7), kind=kCustom, calls=%fused_computation.3.clone | custom fusion | bytes 1572960 | tf_op jit(solution)/shard_map/jit(_take)/gather | solution.py:47
  74.6 2.4 %gather_fusion.2 = f32[96,64,128]{2,1,0:T(8,128)} fusion(f32[16,64,128]{2,1,0:T(8,128)S(1)} %bitcast.119, s32[1024]{0:T(1024)S(1)} %get-tuple-element.35), kind=kCustom, calls=%fused_computation.2.clone | custom fusion | bytes 6291840 | tf_op jit(solution)/shard_map/jit(_take)/gather | solution.py:55
  77.0 1.4 %bitcast_select_fusion.2 = f32[1,24,64,128]{3,2,1,0:T(8,128)S(1)} fusion(f32[24,64,128]{2,1,0:T(8,128)} %gather_fusion.3, pred[24]{0:T(512)(128)(4,1)S(1)} %copy-done.12), kind=kLoop, calls=%fused_computation.14 | loop fusion | flops 196608 | bytes 1572888 | tf_op jit(solution)/shard_map/jit(_take)/select_n | solution.py:47
  78.4 0.1 broadcast_multiply_fusion
  78.5 0.1 slice_bitcast_fusion
  78.5 0.1 collective-permute-start.13
  78.6 2.6 %collective-permute-start.12 = (f32[1,4,64,128]{3,2,1,0:T(8,128)S(1)}, f32[1,4,64,128]{3,2,1,0:T(8,128)S(1)}, u32[]{:S(2)}, u32[]{:S(2)}) collective-permute-start(f32[1,4,64,128]{3,2,1,0:T(8,128)S(1)} %get-tuple-element.21), channel_id=1, source_target_pairs={{5,0},{8,1},{9,4},{12,5},{13,8},{0,9},{1,12},{4,13},{7,2},{10,3},{... | collective-permute-start | bytes 393224 | tf_op jit(solution)/shard_map/ppermute | solution.py:21
  81.3 3.8 %collective-permute-start.10 = (f32[1,4,64,128]{3,2,1,0:T(8,128)S(1)}, f32[1,4,64,128]{3,2,1,0:T(8,128)S(1)}, u32[]{:S(2)}, u32[]{:S(2)}) collective-permute-start(f32[1,4,64,128]{3,2,1,0:T(8,128)S(1)} %get-tuple-element.23), channel_id=1, source_target_pairs={{4,0},{5,1},{8,4},{9,5},{12,8},{13,9},{0,12},{1,13},{6,2},{7,3},{1... | collective-permute-start | bytes 393224 | tf_op jit(solution)/shard_map/ppermute | solution.py:21
  85.1 0.3 bitcast_select_fusion
  85.4 6.1 %collective-permute-done.8 = f32[1,4,64,128]{3,2,1,0:T(8,128)S(1)} collective-permute-done((f32[1,4,64,128]{3,2,1,0:T(8,128)S(1)}, f32[1,4,64,128]{3,2,1,0:T(8,128)S(1)}, u32[]{:S(2)}, u32[]{:S(2)}) %collective-permute-start.8) | collective-permute-done | bytes 131104 | tf_op jit(solution)/shard_map/ppermute | solution.py:21
  91.4 1.8 %collective-permute-start.9 = (f32[1,4,64,128]{3,2,1,0:T(8,128)S(1)}, f32[1,4,64,128]{3,2,1,0:T(8,128)S(1)}, u32[]{:S(2)}, u32[]{:S(2)}) collective-permute-start(f32[1,4,64,128]{3,2,1,0:T(8,128)S(1)} %get-tuple-element.24), channel_id=1, source_target_pairs={{13,0},{0,1},{1,4},{4,5},{5,8},{8,9},{9,12},{12,13},{15,2},{2,3},{... | collective-permute-start | bytes 393224 | tf_op jit(solution)/shard_map/ppermute | solution.py:21
  93.3 4.6 %collective-permute-done.9 = f32[1,4,64,128]{3,2,1,0:T(8,128)S(1)} collective-permute-done((f32[1,4,64,128]{3,2,1,0:T(8,128)S(1)}, f32[1,4,64,128]{3,2,1,0:T(8,128)S(1)}, u32[]{:S(2)}, u32[]{:S(2)}) %collective-permute-start.9) | collective-permute-done | bytes 131104 | tf_op jit(solution)/shard_map/ppermute | solution.py:21
  98.0 0.9 convolution_bitcast_fusion
  98.9 0.9 fusion.4
  99.8 0.0 copy-start.3
  99.8 2.6 %fusion.3 = f32[1,16,64,128]{3,2,1,0:T(8,128)S(1)} fusion(f32[16,384,128]{2,1,0:T(8,128)S(1)} %bitcast.120, f32[16,64,384]{2,1,0:T(8,128)S(1)} %copy-done, f32[64,128,16]{1,2,0:T(8,128)S(1)} %fusion.4, f32[1,16,64,128]{3,2,1,0:T(8,128)S(1)} %multiply_subtract_fusion.2, f32[16,64]{1,0:T(8,128)S(1)} %broadcast_add_fusion), kind=kOutput, calls=%fused_computation.13 | convolution fusion | flops 604372992 | bytes 6295552 | tf_op jit(solution)/shard_map/nik,hnkp->hnip/dot_general | solution.py:59
  102.4 1.3 collective-permute-start.15
  103.7 4.6 %collective-permute-start.14 = (f32[1,16,64,128]{3,2,1,0:T(8,128)S(1)}, f32[1,16,64,128]{3,2,1,0:T(8,128)S(1)}, u32[]{:S(2)}, u32[]{:S(2)}) collective-permute-start(f32[1,16,64,128]{3,2,1,0:T(8,128)S(1)} %fusion.3), channel_id=1, source_target_pairs={{0,2},{1,3},{4,6},{5,7},{8,10},{9,11},{12,14},{13,15},{16,18},{17,... | collective-permute-start | bytes 1572872 | tf_op jit(solution)/shard_map/ppermute | solution.py:31
  108.3 7.2 %collective-permute-done.15 = f32[1,16,64,128]{3,2,1,0:T(8,128)S(1)} collective-permute-done((f32[1,16,64,128]{3,2,1,0:T(8,128)S(1)}, f32[1,16,64,128]{3,2,1,0:T(8,128)S(1)}, u32[]{:S(2)}, u32[]{:S(2)}) %collective-permute-start.15) | collective-permute-done | bytes 524320 | tf_op jit(solution)/shard_map/ppermute | solution.py:32
  115.5 1.2 collective-permute-done.14
  116.7 1.0 multiply_reduce_fusion
  117.7 6.0 %all-reduce = (f32[128]{0:T(128)S(1)}, f32[128]{0:T(128)S(1)}) all-reduce(f32[128]{0:T(128)S(1)} %get-tuple-element.5, f32[128]{0:T(128)S(1)} %get-tuple-element.4), channel_id=1, replica_groups=mesh['grp'=2,'mesh'=4,'tm'=2,'rep'=2] {'tm','rep'}, use_global_device_ids=true, to_apply=%region_7.10 | all-reduce | flops 256 | bytes 2048 | tf_op jit(solution)/shard_map/psum | solution.py:11
  123.7 11.8 %all-reduce.2 = (f32[128]{0:T(128)S(1)}, f32[128]{0:T(128)S(1)}) all-reduce(f32[128]{0:T(128)S(1)} %get-tuple-element.8, f32[128]{0:T(128)S(1)} %get-tuple-element.9), channel_id=1, replica_groups=mesh['grp'=2,'mesh'=4,'tm'=2,'rep'=2] {'mesh'}, use_global_device_ids=true, to_apply=%region_8.11 | all-reduce | flops 256 | bytes 2048 | tf_op jit(solution)/shard_map/psum | solution.py:11
  135.5 2.2 %multiply_subtract_fusion = (f32[1,16,64,128]{3,2,1,0:T(8,128)}, f32[1,16,64,128]{3,2,1,0:T(8,128)}) fusion(f32[1,16,64,128]{3,2,1,0:T(8,128)S(1)} %multiply_subtract_fusion.2, f32[1,16,64,128]{3,2,1,0:T(8,128)} %get-tuple-element.18, f32[1,16,64,128]{3,2,1,0:T(8,128)S(1)} %copy-done.3, f32[128]{0:T(128)S(1)} %get-tuple-element.17, ...), kind=kLoop, calls=%fused_computation.22 | loop fusion | flops 1179648 | bytes 3147264 | tf_op jit(solution)/shard_map/sub | solution.py:140
  (50 shorter events, 0.2 us)
Async XLA Ops:
  0.6 34.3 %copy-start = (f32[16,64,384]{2,1,0:T(8,128)S(1)}, f32[16,64,384]{2,1,0:T(8,128)}, u32[]{:S(2)}) copy-start(f32[16,64,384]{2,1,0:T(8,128)} %param.15) | copy-start | bytes 4718596
  1.6 0.5 copy-start.8
  1.6 4.0 %copy-start.11 = (pred[24]{0:T(512)(128)(4,1)}, pred[24]{0:T(512)(128)(4,1)S(1)}, u32[]{:S(2)}) copy-start(pred[24]{0:T(512)(128)(4,1)S(1)} %compare_and_fusion) | copy-start | bytes 76
  3.7 1.9 %copy-start.7 = (s32[1024]{0:T(1024)}, s32[1024]{0:T(1024)S(1)}, u32[]{:S(2)}) copy-start(s32[1024]{0:T(1024)S(1)} %get-tuple-element.34) | copy-start | bytes 12292
  3.7 11.2 %copy-start.4 = (f32[1,64,1536]{2,1,0:T(8,128)S(1)}, f32[1,64,1536]{2,1,0:T(8,128)}, u32[]{:S(2)}) copy-start(f32[1,64,1536]{2,1,0:T(8,128)} %param.16) | copy-start | bytes 1179652
  5.5 9.6 %copy-start.1 = (f32[1,16,64,128]{3,2,1,0:T(8,128)S(1)}, f32[1,16,64,128]{3,2,1,0:T(8,128)}, u32[]{:S(2)}) copy-start(f32[1,16,64,128]{3,2,1,0:T(8,128)} %param.12) | copy-start | bytes 1572868
  6.5 25.7 %collective-permute-start.5 = (f32[1,4,64,128]{3,2,1,0:T(8,128)S(1)}, f32[1,4,64,128]{3,2,1,0:T(8,128)}, u32[]{:S(2)}, u32[]{:S(2)}) collective-permute-start(f32[1,4,64,128]{3,2,1,0:T(8,128)S(1)} %get-tuple-element.26), channel_id=1, source_target_pairs={{9,0},{12,1},{13,4},{0,5},{1,8},{4,9},{5,12},{8,13},{11,2},{14,3},... | collective-permute-start | bytes 393224 | tf_op jit(solution)/shard_map/ppermute | solution.py:21
  9.0 22.3 %collective-permute-start.4 = (f32[1,4,64,128]{3,2,1,0:T(8,128)S(1)}, f32[1,4,64,128]{3,2,1,0:T(8,128)}, u32[]{:S(2)}, u32[]{:S(2)}) collective-permute-start(f32[1,4,64,128]{3,2,1,0:T(8,128)S(1)} %get-tuple-element.27), channel_id=1, source_target_pairs={{5,0},{8,1},{9,4},{12,5},{13,8},{0,9},{1,12},{4,13},{7,2},{10,3},{... | collective-permute-start | bytes 393224 | tf_op jit(solution)/shard_map/ppermute | solution.py:21
  10.0 20.3 %collective-permute-start.3 = (f32[1,4,64,128]{3,2,1,0:T(8,128)}, f32[1,4,64,128]{3,2,1,0:T(8,128)}, u32[]{:S(2)}, u32[]{:S(2)}) collective-permute-start(f32[1,4,64,128]{3,2,1,0:T(8,128)} %get-tuple-element.28), channel_id=1, source_target_pairs={{12,0},{13,1},{0,4},{1,5},{4,8},{5,9},{8,12},{9,13},{14,2},{15,3},... | collective-permute-start | bytes 393224 | tf_op jit(solution)/shard_map/ppermute | solution.py:21
  12.2 17.2 %collective-permute-start.2 = (f32[1,4,64,128]{3,2,1,0:T(8,128)}, f32[1,4,64,128]{3,2,1,0:T(8,128)}, u32[]{:S(2)}, u32[]{:S(2)}) collective-permute-start(f32[1,4,64,128]{3,2,1,0:T(8,128)} %get-tuple-element.29), channel_id=1, source_target_pairs={{4,0},{5,1},{8,4},{9,5},{12,8},{13,9},{0,12},{1,13},{6,2},{7,3},{1... | collective-permute-start | bytes 393224 | tf_op jit(solution)/shard_map/ppermute | solution.py:21
  14.2 8.7 %collective-permute-start = (f32[1,4,64,128]{3,2,1,0:T(8,128)}, f32[1,4,64,128]{3,2,1,0:T(8,128)}, u32[]{:S(2)}, u32[]{:S(2)}) collective-permute-start(f32[1,4,64,128]{3,2,1,0:T(8,128)} %get-tuple-element.31), channel_id=1, source_target_pairs={{1,0},{4,1},{5,4},{8,5},{9,8},{12,9},{13,12},{0,13},{3,2},{6,3},{7... | collective-permute-start | bytes 393224 | tf_op jit(solution)/shard_map/ppermute | solution.py:21
  14.9 2.6 %copy-start.13 = (pred[96]{0:T(512)(128)(4,1)}, pred[96]{0:T(512)(128)(4,1)S(1)}, u32[]{:S(2)}) copy-start(pred[96]{0:T(512)(128)(4,1)S(1)} %compare_and_fusion.1) | copy-start | bytes 292
  17.5 2.2 %copy-start.6 = (f32[16,64]{1,0:T(8,128)S(1)}, f32[16,64]{1,0:T(8,128)}, u32[]{:S(2)}) copy-start(f32[16,64]{1,0:T(8,128)} %param.13) | copy-start | bytes 12292
  17.5 5.4 %copy-start.5 = (f32[1,4,64,128]{3,2,1,0:T(8,128)S(1)}, f32[1,4,64,128]{3,2,1,0:T(8,128)}, u32[]{:S(2)}) copy-start(f32[1,4,64,128]{3,2,1,0:T(8,128)} %get-tuple-element.30) | copy-start | bytes 393220
  19.7 14.3 %copy-start.9 = (s32[24]{0:T(128)S(1)}, s32[24]{0:T(128)}, u32[]{:S(2)}) copy-start(s32[24]{0:T(128)} %copy-done.8) | copy-start | bytes 292
  22.9 6.5 %collective-permute-start.1 = (f32[1,4,64,128]{3,2,1,0:T(8,128)S(1)}, f32[1,4,64,128]{3,2,1,0:T(8,128)S(1)}, u32[]{:S(2)}, u32[]{:S(2)}) collective-permute-start(f32[1,4,64,128]{3,2,1,0:T(8,128)S(1)} %copy-done.5), channel_id=1, source_target_pairs={{13,0},{0,1},{1,4},{4,5},{5,8},{8,9},{9,12},{12,13},{15,2},{2,3},{... | collective-permute-start | bytes 393224 | tf_op jit(solution)/shard_map/ppermute | solution.py:21
  37.5 12.6 %collective-permute-start.7 = (f32[1,16,64,128]{3,2,1,0:T(8,128)S(1)}, f32[1,16,64,128]{3,2,1,0:T(8,128)S(1)}, u32[]{:S(2)}, u32[]{:S(2)}) collective-permute-start(f32[1,16,64,128]{3,2,1,0:T(8,128)S(1)} %fusion.1), channel_id=1, source_target_pairs={{2,0},{3,1},{6,4},{7,5},{10,8},{11,9},{14,12},{15,13},{18,16},{19,... | collective-permute-start | bytes 1572872 | tf_op jit(solution)/shard_map/ppermute | solution.py:32
  38.8 12.5 %collective-permute-start.6 = (f32[1,16,64,128]{3,2,1,0:T(8,128)S(1)}, f32[1,16,64,128]{3,2,1,0:T(8,128)S(1)}, u32[]{:S(2)}, u32[]{:S(2)}) collective-permute-start(f32[1,16,64,128]{3,2,1,0:T(8,128)S(1)} %fusion.1), channel_id=1, source_target_pairs={{0,2},{1,3},{4,6},{5,7},{8,10},{9,11},{12,14},{13,15},{16,18},{17,... | collective-permute-start | bytes 1572872 | tf_op jit(solution)/shard_map/ppermute | solution.py:31
  74.5 2.4 %copy-start.12 = (pred[24]{0:T(512)(128)(4,1)S(1)}, pred[24]{0:T(512)(128)(4,1)}, u32[]{:S(2)}) copy-start(pred[24]{0:T(512)(128)(4,1)} %copy-done.11) | copy-start | bytes 76
  76.9 8.1 %copy-start.2 = (f32[96,64,128]{2,1,0:T(8,128)S(1)}, f32[96,64,128]{2,1,0:T(8,128)}, u32[]{:S(2)}) copy-start(f32[96,64,128]{2,1,0:T(8,128)} %gather_fusion.2) | copy-start | bytes 9437188
  77.0 8.1 %copy-start.14 = (pred[96]{0:T(512)(128)(4,1)S(1)}, pred[96]{0:T(512)(128)(4,1)}, u32[]{:S(2)}) copy-start(pred[96]{0:T(512)(128)(4,1)} %copy-done.13) | copy-start | bytes 292
  78.5 19.4 %collective-permute-start.13 = (f32[1,4,64,128]{3,2,1,0:T(8,128)S(1)}, f32[1,4,64,128]{3,2,1,0:T(8,128)S(1)}, u32[]{:S(2)}, u32[]{:S(2)}) collective-permute-start(f32[1,4,64,128]{3,2,1,0:T(8,128)S(1)} %get-tuple-element.20), channel_id=1, source_target_pairs={{9,0},{12,1},{13,4},{0,5},{1,8},{4,9},{5,12},{8,13},{11,2},{14,3},... | collective-permute-start | bytes 393224 | tf_op jit(solution)/shard_map/ppermute | solution.py:21
  78.6 19.3 %collective-permute-start.12 = (f32[1,4,64,128]{3,2,1,0:T(8,128)S(1)}, f32[1,4,64,128]{3,2,1,0:T(8,128)S(1)}, u32[]{:S(2)}, u32[]{:S(2)}) collective-permute-start(f32[1,4,64,128]{3,2,1,0:T(8,128)S(1)} %get-tuple-element.21), channel_id=1, source_target_pairs={{5,0},{8,1},{9,4},{12,5},{13,8},{0,9},{1,12},{4,13},{7,2},{10,3},{... | collective-permute-start | bytes 393224 | tf_op jit(solution)/shard_map/ppermute | solution.py:21
  81.2 16.7 %collective-permute-start.11 = (f32[1,4,64,128]{3,2,1,0:T(8,128)S(1)}, f32[1,4,64,128]{3,2,1,0:T(8,128)S(1)}, u32[]{:S(2)}, u32[]{:S(2)}) collective-permute-start(f32[1,4,64,128]{3,2,1,0:T(8,128)S(1)} %get-tuple-element.22), channel_id=1, source_target_pairs={{12,0},{13,1},{0,4},{1,5},{4,8},{5,9},{8,12},{9,13},{14,2},{15,3},... | collective-permute-start | bytes 393224 | tf_op jit(solution)/shard_map/ppermute | solution.py:21
  81.3 16.6 %collective-permute-start.10 = (f32[1,4,64,128]{3,2,1,0:T(8,128)S(1)}, f32[1,4,64,128]{3,2,1,0:T(8,128)S(1)}, u32[]{:S(2)}, u32[]{:S(2)}) collective-permute-start(f32[1,4,64,128]{3,2,1,0:T(8,128)S(1)} %get-tuple-element.23), channel_id=1, source_target_pairs={{4,0},{5,1},{8,4},{9,5},{12,8},{13,9},{0,12},{1,13},{6,2},{7,3},{1... | collective-permute-start | bytes 393224 | tf_op jit(solution)/shard_map/ppermute | solution.py:21
  85.1 6.4 %collective-permute-start.8 = (f32[1,4,64,128]{3,2,1,0:T(8,128)S(1)}, f32[1,4,64,128]{3,2,1,0:T(8,128)S(1)}, u32[]{:S(2)}, u32[]{:S(2)}) collective-permute-start(f32[1,4,64,128]{3,2,1,0:T(8,128)S(1)} %get-tuple-element.25), channel_id=1, source_target_pairs={{1,0},{4,1},{5,4},{8,5},{9,8},{12,9},{13,12},{0,13},{3,2},{6,3},{7... | collective-permute-start | bytes 393224 | tf_op jit(solution)/shard_map/ppermute | solution.py:21
  85.4 13.6 %copy-start.10 = (s32[24]{0:T(128)S(1)}, s32[24]{0:T(128)}, u32[]{:S(2)}) copy-start(s32[24]{0:T(128)} %copy-done.8) | copy-start | bytes 292
  91.4 6.4 %collective-permute-start.9 = (f32[1,4,64,128]{3,2,1,0:T(8,128)S(1)}, f32[1,4,64,128]{3,2,1,0:T(8,128)S(1)}, u32[]{:S(2)}, u32[]{:S(2)}) collective-permute-start(f32[1,4,64,128]{3,2,1,0:T(8,128)S(1)} %get-tuple-element.24), channel_id=1, source_target_pairs={{13,0},{0,1},{1,4},{4,5},{5,8},{8,9},{9,12},{12,13},{15,2},{2,3},{... | collective-permute-start | bytes 393224 | tf_op jit(solution)/shard_map/ppermute | solution.py:21
  99.8 35.7 %copy-start.3 = (f32[1,16,64,128]{3,2,1,0:T(8,128)S(1)}, f32[1,16,64,128]{3,2,1,0:T(8,128)}, u32[]{:S(2)}) copy-start(f32[1,16,64,128]{3,2,1,0:T(8,128)} %get-tuple-element.19) | copy-start | bytes 1572868
  102.4 13.1 %collective-permute-start.15 = (f32[1,16,64,128]{3,2,1,0:T(8,128)S(1)}, f32[1,16,64,128]{3,2,1,0:T(8,128)S(1)}, u32[]{:S(2)}, u32[]{:S(2)}) collective-permute-start(f32[1,16,64,128]{3,2,1,0:T(8,128)S(1)} %fusion.3), channel_id=1, source_target_pairs={{2,0},{3,1},{6,4},{7,5},{10,8},{11,9},{14,12},{15,13},{18,16},{19,... | collective-permute-start | bytes 1572872 | tf_op jit(solution)/shard_map/ppermute | solution.py:32
  103.7 13.0 %collective-permute-start.14 = (f32[1,16,64,128]{3,2,1,0:T(8,128)S(1)}, f32[1,16,64,128]{3,2,1,0:T(8,128)S(1)}, u32[]{:S(2)}, u32[]{:S(2)}) collective-permute-start(f32[1,16,64,128]{3,2,1,0:T(8,128)S(1)} %fusion.3), channel_id=1, source_target_pairs={{0,2},{1,3},{4,6},{5,7},{8,10},{9,11},{12,14},{13,15},{16,18},{17,... | collective-permute-start | bytes 1572872 | tf_op jit(solution)/shard_map/ppermute | solution.py:31
